TPU v7x, 32 devices: a whole 2x2x4 slice. The times are simulated.
32 devices in a mesh: groups: 2 (over y), ctx: 4 (over z), mp: 4 (over x, core).
Axes of the slice: x: 2, y: 2, z: 4, core: 2. Of those that a mesh axis runs over, the one named last changes fastest.
Arguments:
- query: bfloat16 [4096, 8192], P(('groups', 'ctx'), 'mp'), parts along dimension 0, may hold values from -200 to 200
- span_keys: bfloat16 [4096, 1024], P(('groups', 'ctx'), 'mp'), parts along dimension 0, may hold values from -6 to 6
- span_values: bfloat16 [4096, 1024], P(('groups', 'ctx'), 'mp'), parts along dimension 0, may hold values from -6 to 6
- cache_keys: bfloat16 [8192, 1024], P(('groups', 'ctx'), 'mp'), parts along dimension 0, may hold values from -13 to 13
- stored_values: bfloat16 [8192, 1024], P(('groups', 'ctx'), 'mp'), parts along dimension 0, may hold values from -6 to 6
- selected: int32 [8, 8, 2], P(('groups', 'ctx'), 'mp'), parts along dimension 0, may hold values from 0 to 7, as said below
Outputs:
- attended: bfloat16 [4096, 8192], P(('groups', 'ctx'), 'mp'), parts along dimension 0
There are 2 independent parts, one for each index of `groups`. A program takes and returns all parts, laid end to end along the dimension named above; each array names one. Nothing has to cross between parts.
Inputs may be any that keep to these rules, and one draw needn't show every extreme that they name: `selected`: the two blocks chosen for a query block and key head lie in different ranges of 2 consecutive blocks, starting at multiples of 2.
All inputs are finite; a program needn't handle non-finite values.
Results may differ from a plain program's by a relative error of at most 0.0047.
Values may be sent and summed in bfloat16 or wider, within the bound.
No kernel may reach another device: no remote copies, remote signals or barrier semaphores. Data moves between devices by JAX's collectives and lax.ppermute only.
A program may use at most 64 MiB of HBM per device.

v0:
```python
import jax
import jax.numpy as jnp
from jax import lax
from jax.sharding import PartitionSpec as P

QUERY_HEADS = 64
KEY_VALUE_HEADS = 8
HEAD_DIMENSION = 128


def attend(query_group, all_keys, all_values, query_group_count):
    block_rows = query_group.shape[0]
    head_size = all_keys.shape[1]
    score_scale = head_size ** (-0.5)
    query_pos = jnp.arange(block_rows, dtype=jnp.int32)[:, None]
    key_pos = jnp.arange(all_keys.shape[0], dtype=jnp.int32)[None, :]
    visible = (key_pos >= block_rows) | (key_pos <= query_pos)
    results = []
    for member in range(query_group_count):
        query_head = query_group[:, member * head_size : (member + 1) * head_size]
        scores = jnp.dot(query_head, all_keys.T, preferred_element_type=jnp.float32) * score_scale
        scores = jnp.where(visible, scores, jnp.float32(-1e30))
        maxima = jnp.max(scores, axis=1, keepdims=True)
        exponent = jnp.exp(scores - maxima)
        denominator = jnp.sum(exponent, axis=1, keepdims=True)
        weights = (exponent / denominator).astype(jnp.bfloat16)
        results.append(
            jnp.dot(weights, all_values, preferred_element_type=jnp.float32).astype(jnp.bfloat16)
        )
    return jnp.concatenate(results, axis=1)


def per_device(query, span_keys, span_values, cache_keys, stored_values, selected):
    block_rows = query.shape[0]
    head_size = HEAD_DIMENSION
    kv_local = span_keys.shape[1] // head_size
    query_group_count = QUERY_HEADS // KEY_VALUE_HEADS
    wanted = selected[0]
    initial = jnp.zeros((kv_local, 2, block_rows, 2 * head_size), jnp.bfloat16)
    begin_row = jnp.int32(0)
    key_piece = lax.all_gather(cache_keys, "ctx", axis=0, tiled=True)
    value_piece = lax.all_gather(stored_values, "ctx", axis=0, tiled=True)
    piece_rows = key_piece.shape[0]
    updated = initial
    for collect_key_value_head in range(kv_local):
        for slot_index in range(2):
            first_row = wanted[collect_key_value_head, slot_index] * block_rows
            inside = (first_row >= begin_row) & (first_row < begin_row + piece_rows)
            offset = jnp.clip(first_row, 0, piece_rows - block_rows)
            key_tile = lax.dynamic_slice(
                key_piece,
                (offset, jnp.int32(collect_key_value_head * head_size)),
                (block_rows, head_size),
            )
            value_tile = lax.dynamic_slice(
                value_piece,
                (offset, jnp.int32(collect_key_value_head * head_size)),
                (block_rows, head_size),
            )
            tile_block = jnp.concatenate([key_tile, value_tile], axis=1)
            updated = updated.at[collect_key_value_head, slot_index].set(
                jnp.where(inside, tile_block, updated[collect_key_value_head, slot_index])
            )
    results = []
    for key_value_head in range(kv_local):
        query_group = query[
            :,
            key_value_head
            * query_group_count
            * head_size : (key_value_head + 1)
            * query_group_count
            * head_size,
        ]
        all_keys = jnp.concatenate(
            [
                span_keys[:, key_value_head * head_size : (key_value_head + 1) * head_size],
                updated[key_value_head, 0, :, :head_size],
                updated[key_value_head, 1, :, :head_size],
            ],
            axis=0,
        )
        all_values = jnp.concatenate(
            [
                span_values[:, key_value_head * head_size : (key_value_head + 1) * head_size],
                updated[key_value_head, 0, :, head_size:],
                updated[key_value_head, 1, :, head_size:],
            ],
            axis=0,
        )
        results.append(attend(query_group, all_keys, all_values, query_group_count))
    return jnp.concatenate(results, axis=1)


def solution(mesh):
    in_specs = (
        P(("groups", "ctx"), "mp"),
        P(("groups", "ctx"), "mp"),
        P(("groups", "ctx"), "mp"),
        P(("groups", "ctx"), "mp"),
        P(("groups", "ctx"), "mp"),
        P(("groups", "ctx"), "mp", None),
    )
    out_specs = P(("groups", "ctx"), "mp")
    return jax.shard_map(
        per_device, mesh=mesh, in_specs=in_specs, out_specs=out_specs, check_vma=False
    )
```

profile of v0, /device:TPU:0, one launch (start us, length us, event | category | flops | bytes accessed | tf_op | source)
XLA Modules:
  0.0 166.1 jit_solution(3036520839376949744)
XLA Ops:
  6.5 0.7 all-gather.5.cloned.1.call-update
  8.0 1.4 fusion.116
  12.7 1.0 fusion.115
  13.7 1.0 fusion.114
  14.7 42.9 %all-gather.5.cloned.1.call-done = bf16[4096,256]{1,0:T(8,128)(2,1)} async-done(((bf16[1024,256]{1,0:T(8,128)(2,1)}), bf16[4096,256]{1,0:T(8,128)(2,1)}) %all-gather.5.cloned.1.call-update) | async-done | bytes 2097168 | tf_op jit(solution)/shard_map/all_gather | solution.py:42
  57.6 1.2 dynamic-slice_bitcast_fusion.2
  58.8 45.0 %all-gather.3.cloned.1.call-done = bf16[4096,256]{1,0:T(8,128)(2,1)} async-done(((bf16[1024,256]{1,0:T(8,128)(2,1)}), bf16[4096,256]{1,0:T(8,128)(2,1)}) %all-gather.3.cloned.1.call-update) | async-done | bytes 2097168 | tf_op jit(solution)/shard_map/all_gather | solution.py:41
  103.9 1.2 dynamic-slice_bitcast_fusion.3
  105.2 1.3 fusion.97
  106.5 0.8 slice_bitcast_fusion.5
  107.3 5.6 %fusion.118 = (f32[512]{0:T(512)}, f32[512,1536]{0,1:T(8,128)}) fusion(bf16[512,2048]{1,0:T(8,128)(2,1)} %param.14, bf16[512,128]{1,0:T(8,128)(2,1)S(1)} %get-tuple-element.65, bf16[512,128]{1,0:T(8,128)(2,1)S(1)} %get-tuple-element.66, bf16[512,128]{1,0:T(8,128)(2,1)S(1)} %get-tuple-element.74, pred[1536]{0:T(1024)(128)(4,1)S(1)} %iota_compare_fusion.1), kind=kOutput, calls=%fused_computation.192 | convolution fusion | flops 206437888 | bytes 3673600 | tf_op jit(solution)/shard_map/dot_general | solution.py:21
  112.9 1.2 fusion.119
  114.1 1.2 fusion.120
  115.2 1.2 fusion.121
  116.4 1.2 fusion.122
  117.6 1.2 fusion.123
  118.8 1.2 fusion.124
  120.9 1.2 fusion.126
  122.1 1.2 fusion.127
  123.3 1.2 fusion.128
  124.5 1.2 fusion.129
  127.6 1.3 fusion.133
  128.9 3.0 %fusion.33 = f32[512]{0:T(512)} fusion(f32[512,1536]{0,1:T(8,128)} %get-tuple-element.82, f32[512]{0:T(512)} %get-tuple-element.81), kind=kLoop, calls=%fused_computation.82 | loop fusion | flops 1572352 | bytes 3149824 | tf_op jit(solution)/shard_map/reduce_sum | solution.py:25
  131.9 1.8 %fusion.34 = f32[512]{0:T(512)} fusion(f32[512,1536]{0,1:T(8,128)S(1)} %get-tuple-element.84, f32[512]{0:T(512)} %get-tuple-element.83), kind=kLoop, calls=%fused_computation.83 | loop fusion | flops 1572352 | bytes 3149824 | tf_op jit(solution)/shard_map/reduce_sum | solution.py:25
  133.7 3.3 %fusion.81 = bf16[512,2048]{0,1:T(8,128)(2,1)} fusion(f32[512,1536]{0,1:T(8,128)} %get-tuple-element.82, f32[512]{0:T(512)} %fusion.33, f32[512]{0:T(512)} %get-tuple-element.81, bf16[512,128]{1,0:T(8,128)(2,1)S(1)} %copy-done.2, bf16[512,128]{1,0:T(8,128)(2,1)S(1)} %copy-done.1, bf16[512,128]{1,0:T(8,128)(2,1)S(1)} %get-tuple-element.68), kind=kOutput, calls=%fused_computation.130 | convolution fusion | flops 204931072 | bytes 3674112 | tf_op jit(solution)/shard_map/dot_general | solution.py:28
  137.0 1.3 fusion.82
  138.3 1.3 fusion.35
  139.9 0.9 fusion.83
  146.2 0.7 fusion.88
  148.8 0.7 fusion.90
  153.1 0.8 fusion.46
  156.9 2.4 %copy.7 = bf16[512,2048]{1,0:T(8,128)(2,1)} copy(bf16[512,2048]{0,1:T(8,128)(2,1)S(1)} %fusion.96) | data formatting | bytes 4194304 | tf_op jit(solution)/shard_map/concatenate | solution.py:91
  (69 shorter events, 18.3 us)
Async XLA Ops:
  6.5 51.1 %all-gather.5.cloned.1.call-start = ((), (), s32[]{:S(2)}) async-start(), calls=%async_computation.1 | async-start | bytes 2621440 | tf_op jit(solution)/shard_map/all_gather | solution.py:42
  7.3 96.6 %all-gather.3.cloned.1.call-start = ((), (), s32[]{:S(2)}) async-start(), calls=%async_computation | async-start | bytes 2621440 | tf_op jit(solution)/shard_map/all_gather | solution.py:41
  12.1 114.9 %copy-start.14 = (pred[1536]{0:T(1024)(128)(4,1)}, pred[1536]{0:T(1024)(128)(4,1)S(1)}, u32[]{:S(2)}) copy-start(pred[1536]{0:T(1024)(128)(4,1)S(1)} %iota_compare_fusion.1) | copy-start | bytes 4612
  106.5 6.4 %copy-start.15 = (bf16[512,2048]{1,0:T(8,128)(2,1)S(1)}, bf16[512,2048]{1,0:T(8,128)(2,1)}, u32[]{:S(2)}) copy-start(bf16[512,2048]{1,0:T(8,128)(2,1)} %param.14) | copy-start | bytes 6291460
  128.9 4.8 %copy-start.1 = (bf16[512,128]{1,0:T(8,128)(2,1)S(1)}, bf16[512,128]{1,0:T(8,128)(2,1)}, u32[]{:S(2)}) copy-start(bf16[512,128]{1,0:T(8,128)(2,1)} %get-tuple-element.63) | copy-start | bytes 393220
  128.9 4.8 %copy-start.2 = (bf16[512,128]{1,0:T(8,128)(2,1)S(1)}, bf16[512,128]{1,0:T(8,128)(2,1)}, u32[]{:S(2)}) copy-start(bf16[512,128]{1,0:T(8,128)(2,1)} %get-tuple-element.64) | copy-start | bytes 393220
  133.7 3.3 %copy-start.12 = (f32[512]{0:T(512)S(1)}, f32[512]{0:T(512)}, u32[]{:S(2)}) copy-start(f32[512]{0:T(512)} %get-tuple-element.83) | copy-start | bytes 6148
  133.7 3.3 %copy-start.13 = (f32[512]{0:T(512)S(1)}, f32[512]{0:T(512)}, u32[]{:S(2)}) copy-start(f32[512]{0:T(512)} %fusion.34) | copy-start | bytes 6148
  138.3 1.6 copy-start
  138.3 1.6 copy-start.11
  139.9 0.9 copy-start.10
  141.3 0.7 copy-start.8
  142.5 0.7 copy-start.6
  143.7 0.7 copy-start.4
  146.2 0.7 copy-start.9
  146.9 0.7 copy-start.7
  148.7 0.7 copy-start.5
  150.0 0.7 copy-start.3
Sparse Core Ops, SparseCore 0:
  8.9 48.6 all-gather.4
  59.2 44.6 all-gather.2
where the time goes:
time: 167 us; the launch traced here: 166 us
  waiting for transfers between devices  89.3 us (53%)
  matrix products  35.8 us (21%)
  between operations  16.3 us (10%)
  other arithmetic  14.2 us (9%)
  local copies, waits for them, and re-layouts  10.4 us (6%)
    all_gather x1, waiting for transfers between devices, per_device(): key_piece = lax.all_gather(cache_keys, 'ctx', axis=0, tiled=True)  45 us
    all_gather x1, waiting for transfers between devices, per_device(): value_piece = lax.all_gather(stored_values, 'ctx', axis=0, tiled=True)  42.9 us
    dot_general x16, matrix products, attend(): jnp.dot(query_head, all_keys.T, preferred_element_type=jnp.float32)  21.3 us
    dot_general x16, matrix products, attend(): jnp.dot(weights, all_values, preferred_element_type=jnp.float32)  14.5 us
    reduce_sum x16, other arithmetic, attend(): denominator = jnp.sum(exponent, axis=1, keepdims=True)  12.8 us
  transfers between devices with their start and end apart: 2, of which 2 were waited for; matrix products, arithmetic and copies ran while one was open for 3% of the time, Pallas kernels for 0%

commit v1 on v0

--- a/solution.py
+++ b/solution.py
@@ -38,7 +38,12 @@
     wanted = selected[0]
     initial = jnp.zeros((kv_local, 2, block_rows, 2 * head_size), jnp.bfloat16)
     begin_row = jnp.int32(0)
-    key_piece = lax.all_gather(cache_keys, "ctx", axis=0, tiled=True)
+    ring = [cache_keys]
+    for hop in range(3):
+        ring.append(lax.ppermute(ring[-1], "ctx", [(dev, (dev + 1) % 4) for dev in range(4)]))
+    key_piece = jnp.roll(
+        jnp.concatenate(ring[::-1], axis=0), (lax.axis_index("ctx") + 1) * ring[0].shape[0], axis=0
+    )
     value_piece = lax.all_gather(stored_values, "ctx", axis=0, tiled=True)
     piece_rows = key_piece.shape[0]
     updated = initial

time: 167 us -> 144 us (0.86)
  waiting for transfers between devices: 89.3 us -> 52.4 us
  starting transfers between devices: 0.04 us -> 15.4 us
    ppermute x0 -> x3, waiting for transfers between devices: none -> 51.7 us  [per_device(): lax.ppermute(ring[-1], 'ctx', [(dev, (dev + 1) % 4) for dev in range(4)])]
    all_gather x1 -> x0, waiting for transfers between devices: 45 us -> none  [per_device(): key_piece = lax.all_gather(cache_keys, 'ctx', axis=0, tiled=True)]
    all_gather x1, waiting for transfers between devices: 42.9 us -> 0.02 us  [per_device(): value_piece = lax.all_gather(stored_values, 'ctx', axis=0, tiled=True)]
    ppermute x0 -> x3, starting transfers between devices: none -> 15.4 us  [per_device(): lax.ppermute(ring[-1], 'ctx', [(dev, (dev + 1) % 4) for dev in range(4)])]
  transfers between devices with their start and end apart: 2 -> 4, of which waited for: 2 -> 3; matrix products, arithmetic and copies ran while one was open for 3% -> 3% of each run, Pallas kernels for 0% -> 0%
where the time goes in v1:
time: 144 us
  waiting for transfers between devices  52.4 us (36%)
  matrix products  35.9 us (25%)
  between operations  16.3 us (11%)
  starting transfers between devices  15.4 us (11%)
  other arithmetic  14.2 us (10%)
  local copies, waits for them, and re-layouts  9.58 us (7%)
    ppermute x3, waiting for transfers between devices, per_device(): lax.ppermute(ring[-1], 'ctx', [(dev, (dev + 1) % 4) for dev in range(4)])  51.7 us
    dot_general x16, matrix products, attend(): jnp.dot(query_head, all_keys.T, preferred_element_type=jnp.float32)  21.3 us
    ppermute x3, starting transfers between devices, per_device(): lax.ppermute(ring[-1], 'ctx', [(dev, (dev + 1) % 4) for dev in range(4)])  15.4 us
    dot_general x16, matrix products, attend(): jnp.dot(weights, all_values, preferred_element_type=jnp.float32)  14.5 us
    reduce_sum x16, other arithmetic, attend(): denominator = jnp.sum(exponent, axis=1, keepdims=True)  12.7 us
  transfers between devices with their start and end apart: 4, of which 3 were waited for; matrix products, arithmetic and copies ran while one was open for 3% of the time, Pallas kernels for 0%

profile of v1, /device:TPU:0, one launch (start us, length us, event | category | flops | bytes accessed | tf_op | source)
XLA Modules:
  0.0 143.8 jit_solution(3926737834950121380)
XLA Ops:
  7.3 3.1 %collective-permute-start = (bf16[1024,256]{1,0:T(8,128)(2,1)}, bf16[1024,256]{1,0:T(8,128)(2,1)S(1)}, u32[]{:S(2)}, u32[]{:S(2)}) collective-permute-start(bf16[1024,256]{1,0:T(8,128)(2,1)} %param.17), channel_id=1, source_target_pairs={{0,4},{4,8},{8,12},{12,0},{1,5},{5,9},{9,13},{13,1},{2,6},{6,10},{... | collective-permute-start | bytes 1572872 | tf_op jit(solution)/shard_map/ppermute | solution.py:43
  10.3 15.3 %collective-permute-done = bf16[1024,256]{1,0:T(8,128)(2,1)S(1)} collective-permute-done((bf16[1024,256]{1,0:T(8,128)(2,1)}, bf16[1024,256]{1,0:T(8,128)(2,1)S(1)}, u32[]{:S(2)}, u32[]{:S(2)}) %collective-permute-start) | collective-permute-done | bytes 524320 | tf_op jit(solution)/shard_map/ppermute | solution.py:43
  25.7 3.0 %collective-permute-start.1 = (bf16[1024,256]{1,0:T(8,128)(2,1)S(1)}, bf16[1024,256]{1,0:T(8,128)(2,1)S(1)}, u32[]{:S(2)}, u32[]{:S(2)}) collective-permute-start(bf16[1024,256]{1,0:T(8,128)(2,1)S(1)} %collective-permute-done), channel_id=1, source_target_pairs={{0,4},{4,8},{8,12},{12,0},{1,5},{5,9},{9,13},{13,1},{2,6},{6,10},{... | collective-permute-start | bytes 1572872 | tf_op jit(solution)/shard_map/ppermute | solution.py:43
  28.7 1.4 %fusion.116 = (s32[1,1]{1,0:T(1,128)}, s32[1,1]{1,0:T(1,128)}, s32[1,1]{1,0:T(1,128)}, s32[1,1]{1,0:T(1,128)}) fusion(s32[2,2]{1,0:T(2,128)} %bitcast.107), kind=kLoop, calls=%fused_computation.198 | loop fusion | bytes 32 | tf_op jit(solution)/shard_map/slice | solution.py:52
  33.3 21.7 %collective-permute-done.1 = bf16[1024,256]{1,0:T(8,128)(2,1)S(1)} collective-permute-done((bf16[1024,256]{1,0:T(8,128)(2,1)S(1)}, bf16[1024,256]{1,0:T(8,128)(2,1)S(1)}, u32[]{:S(2)}, u32[]{:S(2)}) %collective-permute-start.1) | collective-permute-done | bytes 524320 | tf_op jit(solution)/shard_map/ppermute | solution.py:43
  55.1 9.3 %collective-permute-start.2 = (bf16[1024,256]{1,0:T(8,128)(2,1)S(1)}, bf16[1024,256]{1,0:T(8,128)(2,1)S(1)}, u32[]{:S(2)}, u32[]{:S(2)}) collective-permute-start(bf16[1024,256]{1,0:T(8,128)(2,1)S(1)} %collective-permute-done.1), channel_id=1, source_target_pairs={{0,4},{4,8},{8,12},{12,0},{1,5},{5,9},{9,13},{13,1},{2,6},{6,10},{... | collective-permute-start | bytes 1572872 | tf_op jit(solution)/shard_map/ppermute | solution.py:43
  64.4 1.0 fusion.115
  65.4 1.0 fusion.114
  66.4 14.6 %collective-permute-done.2 = bf16[1024,256]{1,0:T(8,128)(2,1)S(1)} collective-permute-done((bf16[1024,256]{1,0:T(8,128)(2,1)S(1)}, bf16[1024,256]{1,0:T(8,128)(2,1)S(1)}, u32[]{:S(2)}, u32[]{:S(2)}) %collective-permute-start.2) | collective-permute-done | bytes 524320 | tf_op jit(solution)/shard_map/ppermute | solution.py:43
  81.5 1.3 dynamic-slice_bitcast_fusion.2
  82.9 1.3 fusion.97
  84.2 0.8 slice_bitcast_fusion.5
  85.0 5.6 %fusion.118 = (f32[512]{0:T(512)}, f32[512,1536]{0,1:T(8,128)}) fusion(bf16[512,2048]{1,0:T(8,128)(2,1)} %param.14, bf16[512,128]{1,0:T(8,128)(2,1)S(1)} %get-tuple-element.65, bf16[512,128]{1,0:T(8,128)(2,1)S(1)} %get-tuple-element.66, bf16[512,128]{1,0:T(8,128)(2,1)S(1)} %get-tuple-element.74, pred[1536]{0:T(1024)(128)(4,1)S(1)} %iota_compare_fusion.1), kind=kOutput, calls=%fused_computation.200 | convolution fusion | flops 206437888 | bytes 3673600 | tf_op jit(solution)/shard_map/dot_general | solution.py:21
  90.6 1.2 fusion.119
  91.7 1.2 fusion.120
  92.9 1.2 fusion.121
  94.1 1.2 fusion.122
  95.3 1.2 fusion.123
  96.5 1.2 fusion.124
  98.6 1.2 fusion.126
  99.8 1.2 fusion.127
  101.0 1.2 fusion.128
  102.2 1.2 fusion.129
  105.3 1.3 fusion.133
  106.6 3.0 %fusion.33 = f32[512]{0:T(512)} fusion(f32[512,1536]{0,1:T(8,128)} %get-tuple-element.82, f32[512]{0:T(512)} %get-tuple-element.81), kind=kLoop, calls=%fused_computation.82 | loop fusion | flops 1572352 | bytes 3149824 | tf_op jit(solution)/shard_map/reduce_sum | solution.py:25
  109.6 1.7 %fusion.34 = f32[512]{0:T(512)} fusion(f32[512,1536]{0,1:T(8,128)S(1)} %get-tuple-element.84, f32[512]{0:T(512)} %get-tuple-element.83), kind=kLoop, calls=%fused_computation.83 | loop fusion | flops 1572352 | bytes 3149824 | tf_op jit(solution)/shard_map/reduce_sum | solution.py:25
  111.3 3.3 %fusion.81 = bf16[512,2048]{0,1:T(8,128)(2,1)} fusion(f32[512,1536]{0,1:T(8,128)} %get-tuple-element.82, f32[512]{0:T(512)} %fusion.33, f32[512]{0:T(512)} %get-tuple-element.81, bf16[512,128]{1,0:T(8,128)(2,1)S(1)} %copy-done.3, bf16[512,128]{1,0:T(8,128)(2,1)S(1)} %copy-done.2, bf16[512,128]{1,0:T(8,128)(2,1)S(1)} %get-tuple-element.68), kind=kOutput, calls=%fused_computation.130 | convolution fusion | flops 204931072 | bytes 3674112 | tf_op jit(solution)/shard_map/dot_general | solution.py:28
  114.6 1.3 fusion.82
  115.9 1.3 fusion.35
  117.5 0.9 fusion.83
  130.7 0.8 fusion.46
  134.5 2.4 %copy.7 = bf16[512,2048]{1,0:T(8,128)(2,1)} copy(bf16[512,2048]{0,1:T(8,128)(2,1)S(1)} %fusion.96) | data formatting | bytes 4194304 | tf_op jit(solution)/shard_map/concatenate | solution.py:96
  (82 shorter events, 20.1 us)
Async XLA Ops:
  6.5 74.5 %copy-start.1 = (bf16[1024,256]{1,0:T(8,128)(2,1)S(1)}, bf16[1024,256]{1,0:T(8,128)(2,1)}, u32[]{:S(2)}) copy-start(bf16[1024,256]{1,0:T(8,128)(2,1)} %param.17) | copy-start | bytes 1572868
  6.5 74.9 %all-gather.2.cloned.1.call-start = ((), (), s32[]{:S(2)}) async-start(), calls=%async_computation | async-start | bytes 2621440 | tf_op jit(solution)/shard_map/all_gather | solution.py:47
  7.3 18.4 %collective-permute-start = (bf16[1024,256]{1,0:T(8,128)(2,1)}, bf16[1024,256]{1,0:T(8,128)(2,1)S(1)}, u32[]{:S(2)}, u32[]{:S(2)}) collective-permute-start(bf16[1024,256]{1,0:T(8,128)(2,1)} %param.17), channel_id=1, source_target_pairs={{0,4},{4,8},{8,12},{12,0},{1,5},{5,9},{9,13},{13,1},{2,6},{6,10},{... | collective-permute-start | bytes 1572872 | tf_op jit(solution)/shard_map/ppermute | solution.py:43
  25.7 29.4 %collective-permute-start.1 = (bf16[1024,256]{1,0:T(8,128)(2,1)S(1)}, bf16[1024,256]{1,0:T(8,128)(2,1)S(1)}, u32[]{:S(2)}, u32[]{:S(2)}) collective-permute-start(bf16[1024,256]{1,0:T(8,128)(2,1)S(1)} %collective-permute-done), channel_id=1, source_target_pairs={{0,4},{4,8},{8,12},{12,0},{1,5},{5,9},{9,13},{13,1},{2,6},{6,10},{... | collective-permute-start | bytes 1572872 | tf_op jit(solution)/shard_map/ppermute | solution.py:43
  55.1 25.9 %collective-permute-start.2 = (bf16[1024,256]{1,0:T(8,128)(2,1)S(1)}, bf16[1024,256]{1,0:T(8,128)(2,1)S(1)}, u32[]{:S(2)}, u32[]{:S(2)}) collective-permute-start(bf16[1024,256]{1,0:T(8,128)(2,1)S(1)} %collective-permute-done.1), channel_id=1, source_target_pairs={{0,4},{4,8},{8,12},{12,0},{1,5},{5,9},{9,13},{13,1},{2,6},{6,10},{... | collective-permute-start | bytes 1572872 | tf_op jit(solution)/shard_map/ppermute | solution.py:43
  64.4 40.3 %copy-start.15 = (pred[1536]{0:T(1024)(128)(4,1)}, pred[1536]{0:T(1024)(128)(4,1)S(1)}, u32[]{:S(2)}) copy-start(pred[1536]{0:T(1024)(128)(4,1)S(1)} %iota_compare_fusion.1) | copy-start | bytes 4612
  84.2 6.4 %copy-start.16 = (bf16[512,2048]{1,0:T(8,128)(2,1)S(1)}, bf16[512,2048]{1,0:T(8,128)(2,1)}, u32[]{:S(2)}) copy-start(bf16[512,2048]{1,0:T(8,128)(2,1)} %param.14) | copy-start | bytes 6291460
  106.6 4.7 %copy-start.2 = (bf16[512,128]{1,0:T(8,128)(2,1)S(1)}, bf16[512,128]{1,0:T(8,128)(2,1)}, u32[]{:S(2)}) copy-start(bf16[512,128]{1,0:T(8,128)(2,1)} %get-tuple-element.63) | copy-start | bytes 393220
  106.6 4.7 %copy-start.3 = (bf16[512,128]{1,0:T(8,128)(2,1)S(1)}, bf16[512,128]{1,0:T(8,128)(2,1)}, u32[]{:S(2)}) copy-start(bf16[512,128]{1,0:T(8,128)(2,1)} %get-tuple-element.64) | copy-start | bytes 393220
  111.3 3.3 %copy-start.13 = (f32[512]{0:T(512)S(1)}, f32[512]{0:T(512)}, u32[]{:S(2)}) copy-start(f32[512]{0:T(512)} %get-tuple-element.83) | copy-start | bytes 6148
  111.3 3.3 %copy-start.14 = (f32[512]{0:T(512)S(1)}, f32[512]{0:T(512)}, u32[]{:S(2)}) copy-start(f32[512]{0:T(512)} %fusion.34) | copy-start | bytes 6148
  115.9 1.6 %copy-start = (bf16[512,2048]{0,1:T(8,128)(2,1)S(1)}, bf16[512,2048]{0,1:T(8,128)(2,1)}, u32[]{:S(2)}) copy-start(bf16[512,2048]{0,1:T(8,128)(2,1)} %fusion.82) | copy-start | bytes 6291460
  115.9 1.6 %copy-start.12 = (f32[512]{0:T(512)S(1)}, f32[512]{0:T(512)}, u32[]{:S(2)}) copy-start(f32[512]{0:T(512)} %get-tuple-element.85) | copy-start | bytes 6148
  117.5 0.9 copy-start.11
  118.9 0.7 copy-start.9
  120.1 0.7 copy-start.7
  121.4 0.7 copy-start.5
  123.8 0.7 copy-start.10
  124.5 0.7 copy-start.8
  126.4 0.7 copy-start.6
  127.6 0.7 copy-start.4
Sparse Core Ops, SparseCore 0:
  8.9 64.9 all-gather.1
